TPU v7x, 32 devices: a whole 2x2x4 slice. The times are simulated.
32 devices in a mesh: rep: 2 (over x), seq: 16 (over z, y, core).
Axes of the slice: x: 2, y: 2, z: 4, core: 2. Of those that a mesh axis runs over, the one named last changes fastest.
Arguments:
- cached_keys: bfloat16 [32768, 1024], P(('rep', 'seq')), parts along dimension 0, may hold values from -6 to 6
- cached_values: bfloat16 [32768, 1024], P(('rep', 'seq')), parts along dimension 0, may hold values from -6 to 6
- window_queries: bfloat16 [256, 8192], P(('rep', 'seq')), parts along dimension 0
- kept_count: int32 [32], P(('rep', 'seq')), parts along dimension 0, may hold values from 1 to 640, 8192 in all
- kept_entry: int32 [20480], P(('rep', 'seq')), parts along dimension 0, may hold values from 0 to 8191
- row_owner: int32 [20480], P(('rep', 'seq')), parts along dimension 0, may hold values from 0 to 15, as said below
Outputs:
- importance: float32 [16, 16384], P('rep', 'seq'), parts along dimension 0
- compact_rows: bfloat16 [20480, 256], P(('rep', 'seq')), parts along dimension 0
- compact_score: bfloat16 [20480], P(('rep', 'seq')), parts along dimension 0
There are 2 independent parts, one for each index of `rep`. A program takes and returns all parts, laid end to end along the dimension named above; each array names one. Nothing has to cross between parts.
Inputs may be any that keep to these rules, and one draw needn't show every extreme that they name: `kept_count`: the counts of the 16 devices sum to 8192. `kept_entry`: entries may repeat. `row_owner`: among the 640 slots of one device every owner is named by exactly 40 slots.
All inputs are finite; a program needn't handle non-finite values.
Results may differ from a plain program's by a relative error of at most 0.0004.
Values may be sent and summed in bfloat16 or wider, within the bound.
A program may use at most 64 MiB of HBM per device.

v0:
```python
import jax
import jax.numpy as jnp
from jax import lax
from jax.sharding import PartitionSpec as P

HEADS = 64
KV_HEADS = 8
HEAD_DIM = 128
GROUP = 8
WINDOW = 128
POOL = 7


def joined(shard, axis, combine):
    everything = jax.tree.map(lambda part: lax.all_gather(part, axis), shard)
    initial = jax.tree.map(lambda part: part[0], everything)

    def lap(k, so_far):
        return combine(so_far, jax.tree.map(lambda part: part[k], everything))

    return lax.fori_loop(1, lax.axis_size(axis), lap, initial)


def with_halo(block, sides, width):
    for axis, dim in sides:
        count = lax.axis_size(axis)
        forward = [(i, i + 1) for i in range(count - 1)]
        backward = [(target, source) for source, target in forward]
        low = lax.ppermute(
            lax.slice_in_dim(block, block.shape[dim] - width, None, axis=dim), axis, forward
        )
        high = lax.ppermute(lax.slice_in_dim(block, 0, width, axis=dim), axis, backward)
        block = jnp.concatenate([low, block, high], axis=dim)
    return block


def grouped(piece):
    row_count = piece.shape[0]
    shaped = piece.reshape(row_count, KV_HEADS, GROUP, HEAD_DIM).transpose(1, 2, 0, 3)
    return shaped.reshape(KV_HEADS, GROUP * row_count, HEAD_DIM)


def group_scores(query_rows, key_rows):
    return jnp.einsum(
        "qd,td->qt", query_rows, key_rows, preferred_element_type=jnp.float32
    ) * HEAD_DIM ** (-0.5)


def by_group(stat, row_count):
    return stat.reshape(KV_HEADS, GROUP * row_count)


def combine_stats(earlier, later):
    highest = jnp.maximum(earlier[0], later[0])
    return (
        highest,
        earlier[1] * jnp.exp(earlier[0] - highest) + later[1] * jnp.exp(later[0] - highest),
    )


def per_device(cached_keys, cached_values, window_queries, kept_count, kept_entry, row_owner):
    positions = cached_keys.shape[0]
    peers = lax.axis_size("seq")
    slots = kept_entry.shape[0]
    capacity = slots // peers
    slot_index = jnp.arange(slots, dtype=jnp.int32)
    is_live = slot_index < kept_count[0]
    member = (
        (row_owner[:, None] == jnp.arange(peers, dtype=jnp.int32)[None, :]) & is_live[:, None]
    ).astype(jnp.int32)
    earlier = jnp.cumsum(member, axis=0) - member
    slot_rank = jnp.sum(earlier * member, axis=1)
    head_index = kept_entry // positions
    token_index = kept_entry % positions
    row_index = token_index * KV_HEADS + head_index
    key_rows = cached_keys.reshape(positions * KV_HEADS, HEAD_DIM)[row_index]
    value_rows = cached_values.reshape(positions * KV_HEADS, HEAD_DIM)[row_index]
    payload = jnp.concatenate([key_rows, value_rows], axis=1)
    target = jnp.where(is_live, row_owner * capacity + slot_rank, peers * capacity)
    send_rows = (
        jnp.zeros((peers * capacity, 2 * HEAD_DIM), jnp.bfloat16)
        .at[target]
        .set(payload, mode="drop")
    )
    send_rows = send_rows.reshape(peers, capacity, 2 * HEAD_DIM)
    key_groups = cached_keys.reshape(positions, KV_HEADS, HEAD_DIM).transpose(1, 0, 2)
    whole = lax.all_gather(window_queries, "seq", axis=0, tiled=True)
    blank = jnp.zeros((HEADS, WINDOW), jnp.float32)

    def run_pass(advance, initial):
        return advance(initial, whole, 0)

    def both_pass(carry, piece, start):
        row_count = piece.shape[0]

        def local_stats(operands):
            scores = group_scores(operands[0], operands[1])
            peak_rows = jnp.max(scores, axis=1)
            return (peak_rows, jnp.sum(jnp.exp(scores - peak_rows[:, None]), axis=1))

        peaks, totals = lax.map(local_stats, (grouped(piece), key_groups))
        new_peak = peaks.reshape(HEADS, row_count)
        new_total = totals.reshape(HEADS, row_count)
        return (new_peak, new_total)

    def mass_pass_for(peak_all, inverse):

        def advance(carry, piece, start):
            row_count = piece.shape[0]
            peaks = by_group(peak_all, row_count)
            weights = by_group(inverse, row_count)

            def local_mass(operands):
                scores = group_scores(operands[0], operands[1])
                return jnp.sum(
                    jnp.exp(scores - operands[2][:, None]) * operands[3][:, None], axis=0
                )

            return carry + lax.map(local_mass, (grouped(piece), key_groups, peaks, weights))

        return advance

    local_peak, local_total = run_pass(both_pass, (blank, blank))
    glob_peak, glob_total = joined((local_peak, local_total), "seq", combine_stats)
    inverse = 1.0 / glob_total
    column_mass = run_pass(
        mass_pass_for(glob_peak, inverse), jnp.zeros((KV_HEADS, positions), jnp.float32)
    )
    padded = with_halo(column_mass, (("seq", 1),), POOL // 2)
    pooled = padded[:, 0:positions]
    for offset in range(1, POOL):
        pooled = pooled + padded[:, offset : offset + positions]
    importance = pooled * (peers * positions / (GROUP * WINDOW * POOL))
    score_rows = importance[head_index, token_index].astype(jnp.bfloat16)
    send_score = (
        jnp.zeros((peers * capacity,), jnp.bfloat16).at[target].set(score_rows, mode="drop")
    )
    send_score = send_score.reshape(peers, capacity)
    got_rows, got_score = (
        lax.all_to_all(send_rows, "seq", split_axis=0, concat_axis=0, tiled=True),
        lax.all_to_all(send_score, "seq", split_axis=0, concat_axis=0, tiled=True),
    )
    return (
        importance,
        got_rows.reshape(peers * capacity, 2 * HEAD_DIM),
        got_score.reshape(peers * capacity),
    )


def solution(mesh):
    in_specs = (
        P(("rep", "seq"), None),
        P(("rep", "seq"), None),
        P(("rep", "seq"), None),
        P(("rep", "seq")),
        P(("rep", "seq")),
        P(("rep", "seq")),
    )
    out_specs = (P("rep", "seq"), P(("rep", "seq"), None), P(("rep", "seq")))
    return jax.shard_map(
        per_device, mesh=mesh, in_specs=in_specs, out_specs=out_specs, check_vma=False
    )
```

profile of v0, /device:TPU:0, one launch (start us, length us, event | category | flops | bytes accessed | tf_op | source)
XLA Modules:
  0.0 182.1 jit_solution(3419498139225878264)
XLA Ops:
  11.0 4.3 %reshape.80 = bf16[8192,128]{1,0:T(8,128)(2,1)} reshape(bf16[1024,1024]{1,0:T(8,128)(2,1)} %param.12) | data formatting | bytes 4194304 | tf_op jit(solution)/shard_map/reshape | solution.py:76
  15.3 2.3 %reshape.81 = bf16[8192,128]{1,0:T(8,128)(2,1)} reshape(bf16[1024,1024]{1,0:T(8,128)(2,1)S(1)} %copy-done.2) | data formatting | bytes 4194304 | tf_op jit(solution)/shard_map/reshape | solution.py:77
  17.7 3.7 %gather_fusion = bf16[640,128]{1,0:T(8,128)(2,1)S(1)} fusion(bf16[8192,128]{1,0:T(8,128)(2,1)} %reshape.80, s32[1024]{0:T(1024)S(1)} %pad_clamp_fusion), kind=kCustom, calls=%fused_computation | custom fusion | bytes 330240 | tf_op jit(solution)/shard_map/gather | solution.py:76
  21.4 3.6 %gather_fusion.1 = bf16[640,128]{1,0:T(8,128)(2,1)S(1)} fusion(bf16[8192,128]{1,0:T(8,128)(2,1)} %reshape.81, s32[1024]{0:T(1024)S(1)} %pad_clamp_fusion), kind=kCustom, calls=%fused_computation.1 | custom fusion | bytes 330240 | tf_op jit(solution)/shard_map/gather | solution.py:77
  25.1 6.6 %scatter_custom_fusion = bf16[640,256]{1,0:T(8,128)(2,1)} fusion(s32[640]{0:T(1024)S(1)} %compare_select_fusion.3, bf16[640,128]{1,0:T(8,128)(2,1)S(1)} %gather_fusion.1, bf16[]{:T(256)} %constant.140, bf16[640,128]{1,0:T(8,128)(2,1)S(1)} %gather_fusion, bf16[]{:T(256)} %constant.112.clone.1), kind=kCustom, calls=%fused_computation.26 | custom fusion | flops 655360 | bytes 655364 | tf_op jit(solution)/shard_map/scatter | solution.py:83
  31.7 7.5 %all-to-all-start = ((bf16[16,40,256]{2,1,0:T(8,128)(2,1)}), bf16[16,40,256]{2,1,0:T(8,128)(2,1)S(1)}, u32[]{:S(2)}, u32[]{:S(2)}) async-start(bf16[16,40,256]{2,1,0:T(8,128)(2,1)} %bitcast.22), calls=%async_computation | async-start | bytes 655360 | tf_op jit(solution)/shard_map/all_to_all | solution.py:140
  39.2 2.6 %copy.16 = bf16[1024,1024]{0,1:T(8,128)(2,1)} copy(bf16[1024,1024]{1,0:T(8,128)(2,1)S(1)} %copy-done.1) | data formatting | bytes 4194304 | tf_op args[0]
  41.8 3.0 %copy.18 = bf16[8,1024,128]{2,1,0:T(8,128)(2,1)S(1)} copy(bf16[8,1024,128]{1,2,0:T(8,128)(2,1)} %bitcast.93) | data formatting | bytes 4194304 | tf_op jit(solution)/shard_map/while | solution.py:119
  44.9 12.9 %all-gather.2.cloned.1.call-done = bf16[128,8192]{1,0:T(8,128)(2,1)} async-done(((bf16[8,8192]{1,0:T(8,128)(2,1)}), bf16[128,8192]{1,0:T(8,128)(2,1)}) %all-gather.2.cloned.1.call-update) | async-done | bytes 2097168 | tf_op jit(solution)/shard_map/all_gather | solution.py:87
  57.8 2.2 %copy.22 = bf16[16,8,64,128]{3,2,1,0:T(8,128)(2,1)S(1)} copy(bf16[16,8,64,128]{3,1,2,0:T(8,128)(2,1)} %bitcast.96) | data formatting | bytes 4194304
  60.0 2.7 %copy.15 = bf16[128,8,8,128]{3,0,2,1:T(8,128)(2,1)} copy(bf16[128,8,8,128]{3,2,1,0:T(8,128)(2,1)S(1)} %bitcast.94) | data formatting | bytes 4194304 | tf_op jit(solution)/shard_map/reshape | solution.py:39
  62.7 21.2 %while.39 = (s32[]{:T(128)}, f32[8,1024]{1,0:T(8,128)S(1)}, f32[8,1024]{1,0:T(8,128)S(1)}, bf16[8,1024,128]{2,1,0:T(8,128)(2,1)}, bf16[8,1024,128]{2,1,0:T(8,128)(2,1)S(1)}, /*index=5*/s32[]{:T(128)}, s32[]{:T(128)}) while((s32[]{:T(128)}, f32[8,1024]{1,0:T(8,128)S(1)}, f32[8,1024]{1,0:T(8,128)S(1)}, bf16[8,1024,128]{2,1,0:T(8,128)(2,1)}, ...), condition=%wide.region_3.4_spmd, body=%wide.region_0.3_spmd.sunk | while | flops 273676288 | bytes 8942677 | solution.py:101
  84.0 20.6 %all_gather.11 = f32[16,64,128]{2,1,0:T(8,128)S(1)} all-gather(f32[1,64,128]{2,1,0:T(8,128)S(1)} %all_gather_reshape.7), channel_id=1, replica_groups=mesh['rep'=2,'seq'=16] {'seq'}, dimensions={0}, use_global_device_ids=true | all-gather | bytes 557056 | tf_op jit(solution)/shard_map/all_gather | solution.py:15
  104.6 18.9 %all_gather.10 = f32[16,64,128]{2,1,0:T(8,128)S(1)} all-gather(f32[1,64,128]{2,1,0:T(8,128)S(1)} %all_gather_reshape.6), channel_id=1, replica_groups=mesh['rep'=2,'seq'=16] {'seq'}, dimensions={0}, use_global_device_ids=true | all-gather | bytes 557056 | tf_op jit(solution)/shard_map/all_gather | solution.py:15
  124.4 17.1 %while.41 = (s32[]{:T(128)}, f32[8,1024]{1,0:T(8,128)S(1)}, bf16[8,1024,128]{2,1,0:T(8,128)(2,1)}, bf16[8,1024,128]{2,1,0:T(8,128)(2,1)S(1)}, f32[8,1024]{1,0:T(...) while((s32[]{:T(128)}, f32[8,1024]{1,0:T(8,128)S(1)}, bf16[8,1024,128]{2,1,0:T(8,128)(2,1)}, ...), condition=%wide.region_8.9_spmd, body=%wide.region_6.8_spmd.sunk | while | flops 272628736 | bytes 562269 | solution.py:119
  128.7 2.0 %multiply_reduce_fusion.5 = f32[1024]{0:T(1024)S(1)} fusion(f32[1024]{0:T(1024)S(1)} %bitcast.101, f32[1024]{0:T(1024)S(1)} %bitcast.102, bf16[8,1024,128]{2,1,0:T(8,128)(2,1)S(1)} %get-tuple-element.440, s32[]{:T(128)} %get-tuple-element.429, bf16[8,1024,128]{2,1,0:T(8,128)(2,1)} %get-tuple-element.439), kind=kOutput, calls=%fused_computation.18.clone.1 | convolution fusion | flops 272628736 | bytes 537600 | tf_op jit(solution)/shard_map/while/body/eval_jaxpr/qd,td->qt/dot_general | solution.py:44
  130.8 2.0 %multiply_reduce_fusion.5 = f32[1024]{0:T(1024)S(1)} fusion(f32[1024]{0:T(1024)S(1)} %bitcast.101, f32[1024]{0:T(1024)S(1)} %bitcast.102, bf16[8,1024,128]{2,1,0:T(8,128)(2,1)S(1)} %get-tuple-element.440, s32[]{:T(128)} %get-tuple-element.429, bf16[8,1024,128]{2,1,0:T(8,128)(2,1)} %get-tuple-element.439), kind=kOutput, calls=%fused_computation.18.clone.1 | convolution fusion | flops 272628736 | bytes 537600 | tf_op jit(solution)/shard_map/while/body/eval_jaxpr/qd,td->qt/dot_general | solution.py:44
  132.9 2.0 %multiply_reduce_fusion.5 = f32[1024]{0:T(1024)S(1)} fusion(f32[1024]{0:T(1024)S(1)} %bitcast.101, f32[1024]{0:T(1024)S(1)} %bitcast.102, bf16[8,1024,128]{2,1,0:T(8,128)(2,1)S(1)} %get-tuple-element.440, s32[]{:T(128)} %get-tuple-element.429, bf16[8,1024,128]{2,1,0:T(8,128)(2,1)} %get-tuple-element.439), kind=kOutput, calls=%fused_computation.18.clone.1 | convolution fusion | flops 272628736 | bytes 537600 | tf_op jit(solution)/shard_map/while/body/eval_jaxpr/qd,td->qt/dot_general | solution.py:44
  137.2 2.0 %multiply_reduce_fusion.5 = f32[1024]{0:T(1024)S(1)} fusion(f32[1024]{0:T(1024)S(1)} %bitcast.101, f32[1024]{0:T(1024)S(1)} %bitcast.102, bf16[8,1024,128]{2,1,0:T(8,128)(2,1)S(1)} %get-tuple-element.440, s32[]{:T(128)} %get-tuple-element.429, bf16[8,1024,128]{2,1,0:T(8,128)(2,1)} %get-tuple-element.439), kind=kOutput, calls=%fused_computation.18.clone.1 | convolution fusion | flops 272628736 | bytes 537600 | tf_op jit(solution)/shard_map/while/body/eval_jaxpr/qd,td->qt/dot_general | solution.py:44
  142.8 3.2 %collective-permute-start = (f32[8,3]{1,0:T(8,128)S(1)}, f32[8,3]{1,0:T(8,128)S(1)}, u32[]{:S(2)}, u32[]{:S(2)}) collective-permute-start(f32[8,3]{1,0:T(8,128)S(1)} %get-tuple-element.262), channel_id=1, source_target_pairs={{0,1},{1,2},{2,3},{3,4},{4,5},{5,6},{6,7},{7,8},{8,9},{9,10},{10,1... | collective-permute-start | bytes 296 | tf_op jit(solution)/shard_map/ppermute | solution.py:29
  146.8 4.2 %gather_fusion.2 = bf16[640]{0:T(1024)(128)(2,1)S(1)} fusion(f32[8,1024]{1,0:T(8,128)S(1)} %fusion.31, s32[640]{0:T(1024)S(1)} %get-tuple-element.263), kind=kCustom, calls=%fused_computation.2 | custom fusion | bytes 7680 | tf_op jit(solution)/shard_map/gather | solution.py:134
  151.0 8.6 %scatter_custom_fusion.1 = bf16[640]{0:T(1024)(128)(2,1)S(1)} fusion(s32[640]{0:T(1024)S(1)} %compare_select_fusion.3, bf16[640]{0:T(1024)(128)(2,1)S(1)} %gather_fusion.2, bf16[]{:T(256)} %constant.112.clone.1), kind=kCustom, calls=%fused_computation.81 | custom fusion | bytes 1282 | tf_op jit(solution)/shard_map/scatter | solution.py:136
  160.3 7.1 %all-to-all-start.1 = ((bf16[16,1,40]{2,1,0:T(2,128)(2,1)}), bf16[16,1,40]{2,1,0:T(2,128)(2,1)S(1)}, u32[]{:S(2)}, u32[]{:S(2)}) async-start(bf16[16,1,40]{2,1,0:T(2,128)(2,1)} %all_to_all.12), calls=%async_computation.1 | async-start | bytes 16384 | tf_op jit(solution)/shard_map/all_to_all | solution.py:141
  167.4 6.4 %all-to-all-done.1 = bf16[16,1,40]{2,1,0:T(2,128)(2,1)S(1)} async-done(((bf16[16,1,40]{2,1,0:T(2,128)(2,1)}), bf16[16,1,40]{2,1,0:T(2,128)(2,1)S(1)}, u32[]{:S(2)}, u32[]{:S(2)}) %all-to-all-start.1) | async-done | bytes 1312 | tf_op jit(solution)/shard_map/all_to_all | solution.py:141
  (112 shorter events, 38.7 us)
Async XLA Ops:
  7.2 50.7 %all-gather.2.cloned.1.call-start = ((), (), s32[]{:S(2)}) async-start(), calls=%async_computation.2 | async-start | bytes 2228224 | tf_op jit(solution)/shard_map/all_gather | solution.py:87
  11.0 4.3 %copy-start.2 = (bf16[1024,1024]{1,0:T(8,128)(2,1)S(1)}, bf16[1024,1024]{1,0:T(8,128)(2,1)}, u32[]{:S(2)}) copy-start(bf16[1024,1024]{1,0:T(8,128)(2,1)} %param.13) | copy-start | bytes 6291460
  15.3 2.3 %copy-start.4 = (s32[640]{0:T(1024)S(1)}, s32[640]{0:T(1024)}, u32[]{:S(2)}) copy-start(s32[640]{0:T(1024)} %param.16) | copy-start | bytes 7684
  17.6 7.4 %copy-start.3 = (s32[640]{0:T(1024)S(1)}, s32[640]{0:T(1024)}, u32[]{:S(2)}) copy-start(s32[640]{0:T(1024)} %param.17) | copy-start | bytes 7684
  17.6 21.6 %copy-start.1 = (bf16[1024,1024]{1,0:T(8,128)(2,1)S(1)}, bf16[1024,1024]{1,0:T(8,128)(2,1)}, u32[]{:S(2)}) copy-start(bf16[1024,1024]{1,0:T(8,128)(2,1)} %param.12) | copy-start | bytes 6291460
  31.7 128.6 %all-to-all-start = ((bf16[16,40,256]{2,1,0:T(8,128)(2,1)}), bf16[16,40,256]{2,1,0:T(8,128)(2,1)S(1)}, u32[]{:S(2)}, u32[]{:S(2)}) async-start(bf16[16,40,256]{2,1,0:T(8,128)(2,1)} %bitcast.22), calls=%async_computation | async-start | bytes 655360 | tf_op jit(solution)/shard_map/all_to_all | solution.py:140
  141.5 4.5 %collective-permute-start.1 = (f32[8,3]{1,0:T(8,128)S(1)}, f32[8,3]{1,0:T(8,128)S(1)}, u32[]{:S(2)}, u32[]{:S(2)}) collective-permute-start(f32[8,3]{1,0:T(8,128)S(1)} %get-tuple-element.261), channel_id=1, source_target_pairs={{1,0},{2,1},{3,2},{4,3},{5,4},{6,5},{7,6},{8,7},{9,8},{10,9},{11,1... | collective-permute-start | bytes 296 | tf_op jit(solution)/shard_map/ppermute | solution.py:32
  142.8 3.8 %collective-permute-start = (f32[8,3]{1,0:T(8,128)S(1)}, f32[8,3]{1,0:T(8,128)S(1)}, u32[]{:S(2)}, u32[]{:S(2)}) collective-permute-start(f32[8,3]{1,0:T(8,128)S(1)} %get-tuple-element.262), channel_id=1, source_target_pairs={{0,1},{1,2},{2,3},{3,4},{4,5},{5,6},{6,7},{7,8},{8,9},{9,10},{10,1... | collective-permute-start | bytes 296 | tf_op jit(solution)/shard_map/ppermute | solution.py:29
  146.8 28.5 %copy-start = (f32[8,1024]{1,0:T(8,128)}, f32[8,1024]{1,0:T(8,128)S(1)}, u32[]{:S(2)}) copy-start(f32[8,1024]{1,0:T(8,128)S(1)} %fusion.31) | copy-start | bytes 98308
  160.3 13.5 %all-to-all-start.1 = ((bf16[16,1,40]{2,1,0:T(2,128)(2,1)}), bf16[16,1,40]{2,1,0:T(2,128)(2,1)S(1)}, u32[]{:S(2)}, u32[]{:S(2)}) async-start(bf16[16,1,40]{2,1,0:T(2,128)(2,1)} %all_to_all.12), calls=%async_computation.1 | async-start | bytes 16384 | tf_op jit(solution)/shard_map/all_to_all | solution.py:141
Sparse Core Ops, SparseCore 0:
  10.1 47.6 all-gather.1
where the time goes:
time: 183 us; the launch traced here: 182 us
  local copies, waits for them, and re-layouts  42.4 us (23%)
  blocking collectives  39.5 us (22%)
  matrix products  29.2 us (16%)
  waiting for transfers between devices  20.7 us (11%)
  starting transfers between devices  19.1 us (10%)
  other arithmetic  15.4 us (8%)
  between operations  14.9 us (8%)
    all_gather x2, blocking collectives, joined(): everything = jax.tree.map(lambda part: lax.all_gather(part, axis), shard)  39.5 us
    dot_general x16, matrix products, group_scores(): jnp.einsum('qd,td->qt', query_rows, key_rows, preferred_element_type=jnp....  29.2 us
    all_gather x1, waiting for transfers between devices, per_device(): whole = lax.all_gather(window_queries, 'seq', axis=0, tiled=True)  12.9 us
    scatter x1, local copies, waits for them, and re-layouts, per_device(): jnp.zeros((peers * capacity,), jnp.bfloat16).at[target]  8.61 us
    all_to_all x1, starting transfers between devices, per_device(): lax.all_to_all(send_rows, 'seq', split_axis=0, concat_axis=0, tiled=True)  7.46 us
    all_to_all x1, starting transfers between devices, per_device(): lax.all_to_all(send_score, 'seq', split_axis=0, concat_axis=0, tiled=True)  7.09 us
    scatter x1, other arithmetic, per_device(): send_rows = jnp.zeros((peers * capacity, 2 * HEAD_DIM), jnp.bfloat16).at[...  6.64 us
    all_to_all x1, waiting for transfers between devices, per_device(): lax.all_to_all(send_score, 'seq', split_axis=0, concat_axis=0, tiled=True)  6.44 us
  transfers between devices with their start and end apart: 5, of which 3 were waited for; matrix products, arithmetic and copies ran while one was open for 47% of the time, Pallas kernels for 0%

commit v1 on v0

v1 whole, which is shorter than its diff:
```python
import functools

import jax
import jax.numpy as jnp
from jax import lax
from jax.experimental import pallas as pl
from jax.experimental.pallas import tpu as pltpu
from jax.sharding import PartitionSpec as P

KV_HEADS = 8
GROUP = 8
HEAD_DIM = 128
POOL = 7
LANES = 128
MESH = pl.DeviceIdType.MESH
NT = (((1,), (1,)), ((), ()))


def iota(shape, dim):
    return lax.broadcasted_iota(jnp.int32, shape, dim)


def kernel(
    n, cap, cap_pad, pool_scale,
    keys_hbm, vals_hbm, wq_hbm, count_ref, entry_ref, owner_ref,
    imp_ref, rows_out, score_out,
    keys, vals, qall, ebuf, stat, stat_in, glob, rows_send, onehot, head_hot, mass, halo, ssend, srecv,
    zs, zr, ys, yr, bs, br, ts, tr, gs, gr, rs, rr, hs, hr, ss, sr, ls,
):
    G = KV_HEADS
    me = lax.axis_index("seq")
    A = n // 4
    a, b, c = me // 4, (me // 2) % 2, me % 2
    slots = entry_ref.shape[1]
    positions = keys.shape[0]
    out_slots = n * cap_pad
    qrows = qall.shape[4]
    scale = HEAD_DIM ** (-0.5)
    per_owner = n // G

    def stat_owner(g):
        return (g * per_owner + n // 2) % n

    def to(index):
        return {"seq": index}

    def remote(src, dst, ssem, rsem, index):
        return pltpu.make_async_remote_copy(
            src_ref=src, dst_ref=dst, send_sem=ssem, recv_sem=rsem,
            device_id=to(index), device_id_type=MESH,
        )

    def drain(region, sem):
        pltpu.make_async_copy(region, region, sem).wait()

    key_copy = pltpu.make_async_copy(keys_hbm, keys, ls.at[0])
    val_copy = pltpu.make_async_copy(vals_hbm, vals, ls.at[1])
    own_q = pltpu.make_async_copy(wq_hbm, qall.at[:, c, b, a], ls.at[2])
    own_q.start()
    key_copy.start()
    val_copy.start()
    barrier = pltpu.get_barrier_semaphore()

    @pl.loop(1, n)
    def _(k):
        pl.semaphore_signal(barrier, inc=1, device_id=to(lax.rem(me + k, n)), device_id_type=MESH)

    entry = entry_ref[...]
    owner = owner_ref[...]
    live = iota((1, slots), 1) < count_ref[0]
    owner_live = jnp.where(live, owner, -1)
    member = jnp.where(iota((n, slots), 0) == owner_live, 1.0, 0.0)
    before = jnp.where(iota((slots, slots), 0) < iota((slots, slots), 1), 1.0, 0.0).astype(jnp.bfloat16)
    earlier = jnp.dot(member.astype(jnp.bfloat16), before, preferred_element_type=jnp.float32)
    rank = jnp.sum(member * earlier, axis=0, keepdims=True)
    target = jnp.where(live, owner * cap_pad + rank.astype(jnp.int32), -1)
    head = jnp.zeros((1, slots), jnp.int32)
    for h in range(1, G):
        head = head + jnp.where(entry >= h * positions, 1, 0)
    token = entry - head * positions
    token_f = (token + 1).astype(jnp.float32)
    head_f = head.astype(jnp.float32)
    head_sel = jnp.where(iota((G, slots), 0) == head, 1.0, 0.0).astype(jnp.bfloat16)
    blk = 256
    for i in range(out_slots // blk):
        hit = (iota((blk, slots), 0) + i * blk) == target
        tok = jnp.sum(jnp.where(hit, token_f, 0.0), axis=1, keepdims=True).astype(jnp.int32) - 1
        onehot[i * blk:(i + 1) * blk, :] = jnp.where(
            iota((blk, positions), 1) == tok, 1.0, 0.0
        ).astype(jnp.bfloat16)
        hit_b = jnp.where(hit, 1.0, 0.0).astype(jnp.bfloat16)
        head_hot[:, i * blk:(i + 1) * blk] = lax.dot_general(
            head_sel, hit_b, NT, preferred_element_type=jnp.float32
        )

    own_q.wait()
    pl.semaphore_wait(barrier, n - 1)

    @pl.loop(0, G)
    def _(g):
        @pl.loop(1, A)
        def _(k):
            peer = lax.rem(a + k, A) * 4 + b * 2 + c
            remote(qall.at[g, c, b, a], qall.at[g, c, b, a], zs.at[g], zr.at[g], peer).start()

    key_copy.wait()
    val_copy.wait()

    for i in range(out_slots // blk):
        hit = (iota((blk, slots), 0) + i * blk) == target
        hcol = jnp.sum(jnp.where(hit, head_f, 0.0), axis=1, keepdims=True).astype(jnp.int32)
        hcol = jnp.broadcast_to(hcol, (blk, HEAD_DIM))
        pick = onehot[i * blk:(i + 1) * blk, :]
        for side, source in enumerate((keys, vals)):
            got = jnp.dot(pick, source[...], preferred_element_type=jnp.float32)
            chosen = jnp.zeros((blk, HEAD_DIM), jnp.float32)
            for h in range(G):
                chosen = jnp.where(hcol == h, got[:, h * HEAD_DIM:(h + 1) * HEAD_DIM], chosen)
            rows_send[
                i * blk:(i + 1) * blk,
                side * HEAD_DIM:(side + 1) * HEAD_DIM,
            ] = chosen.astype(jnp.bfloat16)

    def combine(g):
        @pl.when(me == stat_owner(g))
        def _():
            drain(stat_in.at[pl.ds(0, n - 1)], tr.at[0])
            stat_in[me] = stat[g]
            top = stat_in[0, 0]
            for d in range(1, n):
                top = jnp.maximum(top, stat_in[d, 0])
            total = jnp.zeros_like(top)
            for d in range(n):
                total = total + stat_in[d, 1] * jnp.exp(stat_in[d, 0] - top)
            glob[g, 0] = top
            glob[g, 1] = 1.0 / total

            @pl.loop(1, n)
            def _(k):
                remote(glob.at[g], glob.at[g], gs.at[0], gr.at[g], lax.rem(me + k, n)).start()

    chunk = 2 * LANES
    tblk = 256

    def compute(g):
        group_q = qall.at[g].reshape(qall.shape[1] * qall.shape[2] * A * qrows, HEAD_DIM)
        total_rows = group_q.shape[0]
        key_cols = pl.ds(pl.multiple_of(g * HEAD_DIM, HEAD_DIM), HEAD_DIM)

        @pl.loop(0, total_rows // chunk)
        def _(j):
            qs = group_q[pl.ds(pl.multiple_of(j * chunk, chunk), chunk), :]
            lanes = pl.ds(pl.multiple_of(j * chunk, chunk), chunk)
            top8 = None
            for t in range(positions // tblk):
                s = lax.dot_general(
                    keys[t * tblk:(t + 1) * tblk, key_cols], qs, NT, preferred_element_type=jnp.float32
                )
                ebuf[g, t * tblk:(t + 1) * tblk, lanes] = s
                part = jnp.max(s.reshape(tblk // 8, 8, chunk), axis=0)
                top8 = part if top8 is None else jnp.maximum(top8, part)
            top = jnp.max(top8, axis=0, keepdims=True)
            sum8 = jnp.zeros((8, chunk), jnp.float32)
            for t in range(positions // tblk):
                s = ebuf[g, t * tblk:(t + 1) * tblk, lanes]
                e = jnp.exp((s - top) * scale)
                ebuf[g, t * tblk:(t + 1) * tblk, lanes] = e
                sum8 = sum8 + jnp.sum(e.reshape(tblk // 8, 8, chunk), axis=0)
            total = jnp.sum(sum8, axis=0, keepdims=True)
            top = top * scale
            for i in range(chunk // LANES):
                stat[g, 0, pl.ds(j * (chunk // LANES) + i, 1), :] = top[:, i * LANES:(i + 1) * LANES]
                stat[g, 1, pl.ds(j * (chunk // LANES) + i, 1), :] = total[:, i * LANES:(i + 1) * LANES]

        dest = stat_owner(g)

        @pl.when(me != dest)
        def _():
            remote(stat.at[g], stat_in.at[me], ts.at[g], tr.at[0], dest).start()

    mid_peer = a * 4 + (1 - b) * 2 + c
    core_peer = a * 4 + b * 2 + (1 - c)
    lag = 3

    @pl.loop(0, G + lag)
    def _(step):
        @pl.when(step < G)
        def _():
            g = step
            drain(qall.at[g, c, b, pl.ds(0, A - 1)], zr.at[g])
            remote(qall.at[g, c, b], qall.at[g, c, b], ys.at[g], yr.at[g], mid_peer).start()

        @pl.when((step >= 1) & (step < G + 1))
        def _():
            g = step - 1
            drain(qall.at[g, c, 1 - b], yr.at[g])
            remote(qall.at[g, c], qall.at[g, c], bs.at[g], br.at[g], core_peer).start()

        @pl.when((step >= 2) & (step < G + 2))
        def _():
            g = step - 2
            drain(qall.at[g, 1 - c], br.at[g])
            compute(g)

        @pl.when(step >= 3)
        def _():
            combine(step - 3)

    rows3 = rows_send.reshape(n, cap_pad, 2 * HEAD_DIM)

    @pl.loop(1, n)
    def _(k):
        peer = lax.rem(me + k, n)
        remote(rows3.at[peer], rows_out.at[me], rs.at[0], rr.at[0], peer).start()

    own_rows = pltpu.make_async_copy(rows3.at[me], rows_out.at[me], ls.at[3])
    own_rows.start()

    ones = jnp.ones((8, LANES), jnp.float32)

    @pl.loop(0, G)
    def _(g):
        @pl.when(me != stat_owner(g))
        def _():
            drain(glob.at[g], gr.at[g])

        weight = jnp.exp(stat[g, 0] - glob[g, 0]) * glob[g, 1]
        for t in range(positions // LANES):
            acc = ebuf[g, t * LANES:(t + 1) * LANES, 0:LANES] * weight[0:1, :]
            for k in range(1, weight.shape[0]):
                acc = acc + ebuf[g, t * LANES:(t + 1) * LANES, k * LANES:(k + 1) * LANES] * weight[k:k + 1, :]
            line = lax.dot_general(
                ones, acc, NT, preferred_element_type=jnp.float32, precision=lax.Precision.HIGHEST
            )
            mass[g, :, t * LANES:(t + 1) * LANES] = line[0:1, :]

    halo[0] = jnp.zeros((G, LANES), jnp.float32)
    halo[1] = jnp.zeros((G, LANES), jnp.float32)
    column = jnp.concatenate([mass[g] for g in range(G)], axis=0)
    halo[4] = column[:, 0:LANES]
    halo[5] = column[:, positions - LANES:]
    low_copy = remote(halo.at[4], halo.at[3], hs.at[0], hr.at[0], lax.rem(me + n - 1, n))
    high_copy = remote(halo.at[5], halo.at[2], hs.at[1], hr.at[1], lax.rem(me + 1, n))

    @pl.when(me > 0)
    def _():
        low_copy.start()

    @pl.when(me < n - 1)
    def _():
        high_copy.start()

    @pl.when(me > 0)
    def _():
        drain(halo.at[2], hr.at[1])
        halo[0] = halo[2]

    @pl.when(me < n - 1)
    def _():
        drain(halo.at[3], hr.at[0])
        halo[1] = halo[3]

    padded = jnp.concatenate([halo[0], column, halo[1]], axis=1)
    width = padded.shape[1]
    pooled = padded
    for o in range(1, POOL // 2 + 1):
        pooled = pooled + pltpu.roll(padded, o, 1) + pltpu.roll(padded, width - o, 1)
    importance = pooled[:, LANES:LANES + positions] * pool_scale
    imp_ref[...] = importance

    got = lax.dot_general(
        importance.astype(jnp.bfloat16), onehot[...], NT, preferred_element_type=jnp.float32
    )
    line = jnp.sum(got * head_hot[...], axis=0, keepdims=True)
    owner_of = iota((n, out_slots), 1) - iota((n, out_slots), 0) * cap_pad
    spread = jnp.where((owner_of >= 0) & (owner_of < cap_pad), line, 0.0).astype(jnp.bfloat16)
    row_id, lane_id = iota((out_slots, LANES), 0), iota((out_slots, LANES), 1)
    fold = (row_id - lane_id) % cap_pad == 0
    fold = jnp.where(fold & (lane_id < cap_pad), 1.0, 0.0).astype(jnp.bfloat16)
    table = jnp.dot(spread, fold, preferred_element_type=jnp.float32)
    for k in range(n):
        ssend[k] = table[k:k + 1, :]

    @pl.loop(1, n)
    def _(k):
        peer = lax.rem(me + k, n)
        remote(ssend.at[peer], srecv.at[me], ss.at[0], sr.at[0], peer).start()

    own_rows.wait()
    drain(rows_out.at[pl.ds(0, n - 1)], rr.at[0])
    drain(rows3.at[pl.ds(0, n - 1)], rs.at[0])

    @pl.loop(0, G)
    def _(g):
        drain(qall.at[g, c, b, pl.ds(0, A - 1)], zs.at[g])
        drain(qall.at[g, c, b], ys.at[g])
        drain(qall.at[g, c], bs.at[g])

        @pl.when(me != stat_owner(g))
        def _():
            drain(stat.at[g], ts.at[g])

        @pl.when(me == stat_owner(g))
        def _():
            drain(stat_in.at[pl.ds(0, n - 1)], gs.at[0])

    @pl.when(me > 0)
    def _():
        drain(halo.at[4], hs.at[0])

    @pl.when(me < n - 1)
    def _():
        drain(halo.at[5], hs.at[1])

    drain(ssend.at[pl.ds(0, n - 1)], ss.at[0])
    drain(srecv.at[pl.ds(0, n - 1)], sr.at[0])
    srecv[me] = ssend[me]
    score_out[...] = srecv[...]


def per_device(n, cached_keys, cached_values, window_queries, kept_count, kept_entry, row_owner):
    positions, width = cached_keys.shape
    slots = kept_entry.shape[0]
    cap = slots // n
    cap_pad = -(-cap // 16) * 16
    query_rows = window_queries.shape[0]
    heads = window_queries.shape[1] // HEAD_DIM
    group = heads // KV_HEADS
    window = query_rows * n
    qrows = query_rows * group
    lane_rows = n * qrows // LANES
    wq = (
        window_queries.reshape(query_rows, heads, HEAD_DIM)
        .transpose(1, 0, 2)
        .reshape(KV_HEADS, qrows, HEAD_DIM)
    )
    pool_scale = n * positions / (group * window * POOL)
    any_spec = pl.BlockSpec(memory_space=pl.ANY)
    vmem = pl.BlockSpec(memory_space=pltpu.VMEM)
    dma = pltpu.SemaphoreType.DMA
    A = n // 4
    f32, bf16 = jnp.float32, jnp.bfloat16
    importance, rows, score = pl.pallas_call(
        functools.partial(kernel, n, cap, cap_pad, pool_scale),
        out_shape=(
            jax.ShapeDtypeStruct((KV_HEADS, positions), f32),
            jax.ShapeDtypeStruct((n, cap_pad, 2 * HEAD_DIM), bf16),
            jax.ShapeDtypeStruct((n, 1, LANES), f32),
        ),
        in_specs=[any_spec, any_spec, any_spec, pl.BlockSpec(memory_space=pltpu.SMEM), vmem, vmem],
        out_specs=(vmem, any_spec, vmem),
        scratch_shapes=[
            pltpu.VMEM((positions, width), bf16),
            pltpu.VMEM((positions, width), bf16),
            pltpu.VMEM((KV_HEADS, 2, 2, A, qrows, HEAD_DIM), bf16),
            pltpu.VMEM((KV_HEADS, positions, n * qrows), f32),
            pltpu.VMEM((KV_HEADS, 2, lane_rows, LANES), f32),
            pltpu.VMEM((n, 2, lane_rows, LANES), f32),
            pltpu.VMEM((KV_HEADS, 2, lane_rows, LANES), f32),
            pltpu.VMEM((n * cap_pad, 2 * HEAD_DIM), bf16),
            pltpu.VMEM((n * cap_pad, positions), bf16),
            pltpu.VMEM((KV_HEADS, n * cap_pad), f32),
            pltpu.VMEM((KV_HEADS, 1, positions), f32),
            pltpu.VMEM((6, KV_HEADS, LANES), f32),
            pltpu.VMEM((n, 1, LANES), f32),
            pltpu.VMEM((n, 1, LANES), f32),
        ]
        + [dma((KV_HEADS,))] * 6
        + [dma((KV_HEADS,)), dma((1,)), dma((1,)), dma((KV_HEADS,)), dma((1,)), dma((1,))]
        + [dma((2,)), dma((2,)), dma((1,)), dma((1,)), dma((4,))],
        compiler_params=pltpu.CompilerParams(
            collective_id=0, has_side_effects=True, vmem_limit_bytes=60 * 1024 * 1024
        ),
        name="snap",
    )(cached_keys, cached_values, wq, kept_count, kept_entry.reshape(1, slots), row_owner.reshape(1, slots))
    return (
        importance,
        rows[:, :cap].reshape(n * cap, 2 * HEAD_DIM),
        score[:, 0, :cap].reshape(n * cap).astype(bf16),
    )


def solution(mesh):
    n = mesh.shape["seq"]
    split = P(("rep", "seq"))
    wide = P(("rep", "seq"), None)
    return jax.shard_map(
        functools.partial(per_device, n),
        mesh=mesh,
        in_specs=(wide, wide, wide, split, split, split),
        out_specs=(P("rep", "seq"), wide, split),
        check_vma=False,
    )
```

time: 183 us -> 67.3 us (0.37)
  Pallas kernels: 0 us -> 58.6 us
  blocking collectives: 39.5 us -> 0 us
  local copies, waits for them, and re-layouts: 42.4 us -> 7.03 us
  matrix products: 29.2 us -> 0 us
  waiting for transfers between devices: 20.7 us -> 0 us
  starting transfers between devices: 19.1 us -> 0 us
  other arithmetic: 15.4 us -> 0 us
  between operations: 14.9 us -> 1.29 us
    pallas_call x0 -> x1, Pallas kernels: none -> 58.6 us  [per_device(): pl.pallas_call(functools.partial(kernel, n, cap, cap_pad, pool_scale), ou...]
    all_gather x2 -> x0, blocking collectives: 39.5 us -> none  [joined(): everything = jax.tree.map(lambda part: lax.all_gather(part, axis), shard)]
    dot_general x16 -> x0, matrix products: 29.2 us -> none  [group_scores(): jnp.einsum('qd,td->qt', query_rows, key_rows, preferred_element_type=jnp....]
    all_to_all x2 -> x0, starting transfers between devices: 14.6 us -> none  [the longest x1 7.46 us: per_device(): lax.all_to_all(send_rows, 'seq', split_axis=0, concat_axis=0, tiled=True)]
    all_gather x1 -> x0, waiting for transfers between devices: 12.9 us -> none  [per_device(): whole = lax.all_gather(window_queries, 'seq', axis=0, tiled=True)]
    gather x3 -> x0, local copies, waits for them, and re-layouts: 11.5 us -> none  [the longest x1 4.19 us: per_device(): score_rows = importance[head_index, token_index].astype(jnp.bfloat16)]
    scatter x1 -> x0, local copies, waits for them, and re-layouts: 8.61 us -> none  [per_device(): jnp.zeros((peers * capacity,), jnp.bfloat16).at[target]]
    reshape x6 -> x2, local copies, waits for them, and re-layouts: 10 us -> 2.53 us  [the longest x1 1.27 us: per_device(): kept_entry.reshape(1, slots)]
  transfers between devices with their start and end apart: 5 -> 0, of which waited for: 3 -> 0; matrix products, arithmetic and copies ran while one was open for 47% -> 0% of each run, Pallas kernels for 0% -> 0%
where the time goes in v1:
time: 67.3 us; the launch traced here: 67 us
  Pallas kernels  58.6 us (87%)
  local copies, waits for them, and re-layouts  7.03 us (10%)
  between operations  1.29 us (2%)
    pallas_call x1, Pallas kernels, per_device(): pl.pallas_call(functools.partial(kernel, n, cap, cap_pad, pool_scale), ou...  58.6 us
    slice x1, local copies, waits for them, and re-layouts, per_device(): rows[:, :cap].reshape(n * cap, 2 * HEAD_DIM)  1.72 us
    unnamed x1, local copies, waits for them, and re-layouts  1.37 us

profile of v1, /device:TPU:0, one launch (start us, length us, event | category | flops | bytes accessed | tf_op | source)
XLA Modules:
  0.0 67.0 jit_solution(11748321145777855515)
XLA Ops:
  1.3 1.3 %reshape.24.entry_ref = s32[1,640]{1,0:T(1,128)} reshape(s32[640]{0:T(1024)} %param.10) | data formatting | bytes 5120 | tf_op jit(solution)/shard_map/reshape | solution.py:375
  2.5 1.3 %reshape.25.owner_ref = s32[1,640]{1,0:T(1,128)} reshape(s32[640]{0:T(1024)} %param.11) | data formatting | bytes 5120 | tf_op jit(solution)/shard_map/reshape | solution.py:375
  3.8 58.6 %snap.1 = (f32[8,1024]{1,0:T(8,128)}, bf16[16,48,256]{2,1,0:T(8,128)(2,1)}, f32[16,1,128]{2,1,0:T(1,128)}) custom-call(bf16[1024,1024]{1,0:T(8,128)(2,1)} %keys_hbm.1, bf16[1024,1024]{1,0:T(8,128)(2,1)} %vals_hbm.1, bf16[8,64,128]{2,1,0:T(8,128)(2,1)} %bitcast.7, s32[1]{0:T(128)S(6)} %copy.10.count_ref, s32[1,640]{1,0:T(1,128)} %reshape.24.entry_ref, ...), custom_call_target="tpu_custom_call" | custom-call | tf_op jit(solution)/shard_map/snap/pallas_call | solution.py:343
  62.5 0.7 %fusion = bf16[16,40]{1,0:T(8,128)(2,1)S(1)} fusion(f32[16,1,128]{2,1,0:T(1,128)} %get-tuple-element.8), kind=kLoop, calls=%fused_computation.1 | loop fusion | bytes 2560 | tf_op jit(solution)/shard_map/slice | solution.py:379
  63.2 0.7 %convert_element_type.4 = bf16[640]{0:T(1024)(128)(2,1)} reshape(bf16[16,40]{1,0:T(8,128)(2,1)S(1)} %fusion) | data formatting | bytes 2560 | tf_op jit(solution)/shard_map/convert_element_type | solution.py:379
  63.9 1.7 %slice.7 = bf16[16,40,256]{2,1,0:T(8,128)(2,1)} slice(bf16[16,48,256]{2,1,0:T(8,128)(2,1)} %get-tuple-element.7), slice={[0:16], [0:40], [0:256]} | slice | bytes 655360 | tf_op jit(solution)/shard_map/slice | solution.py:378
  65.6 1.4 %copy.11 = f32[8,1024]{1,0:T(8,128)} copy(f32[8,1024]{1,0:T(8,128)} %get-tuple-element.12) | data formatting | bytes 65536

commit v2 on v1

--- a/solution.py
+++ b/solution.py
@@ -11,6 +11,7 @@
 GROUP = 8
 HEAD_DIM = 128
 POOL = 7
+LOG2E = 1.4426950408889634
 LANES = 128
 MESH = pl.DeviceIdType.MESH
 NT = (((1,), (1,)), ((), ()))
@@ -24,14 +25,14 @@
     n, cap, cap_pad, pool_scale,
     keys_hbm, vals_hbm, wq_hbm, count_ref, entry_ref, owner_ref,
     imp_ref, rows_out, score_out,
-    keys, vals, qall, ebuf, stat, stat_in, glob, rows_send, onehot, head_hot, mass, halo, ssend, srecv,
-    zs, zr, ys, yr, bs, br, ts, tr, gs, gr, rs, rr, hs, hr, ss, sr, ls,
+    keys, vals, qall, ebuf, stat, stat_in, stat_all, glob, rows_send, onehot, head_hot, mass, halo, ssend, srecv,
+    zs, zr, ys, yr, bs, br, ts, tr, gs, gr, rs, rr, hs, hr, ss, sr, ls, es, er,
 ):
     G = KV_HEADS
     me = lax.axis_index("seq")
     A = n // 4
     a, b, c = me // 4, (me // 2) % 2, me % 2
-    slots = entry_ref.shape[1]
+    slots = entry_ref.shape[0]
     positions = keys.shape[0]
     out_slots = n * cap_pad
     qrows = qall.shape[4]
@@ -65,8 +66,8 @@
     def _(k):
         pl.semaphore_signal(barrier, inc=1, device_id=to(lax.rem(me + k, n)), device_id_type=MESH)
 
-    entry = entry_ref[...]
-    owner = owner_ref[...]
+    entry = entry_ref[...].reshape(1, slots)
+    owner = owner_ref[...].reshape(1, slots)
     live = iota((1, slots), 1) < count_ref[0]
     owner_live = jnp.where(live, owner, -1)
     member = jnp.where(iota((n, slots), 0) == owner_live, 1.0, 0.0)
@@ -121,19 +122,22 @@
                 side * HEAD_DIM:(side + 1) * HEAD_DIM,
             ] = chosen.astype(jnp.bfloat16)
 
+    def join(g, gathered):
+        gathered[me] = stat[g]
+        top = gathered[0, 0]
+        for d in range(1, n):
+            top = jnp.maximum(top, gathered[d, 0])
+        total = jnp.zeros_like(top)
+        for d in range(n):
+            total = total + gathered[d, 1] * jnp.exp(gathered[d, 0] - top)
+        glob[g, 0] = top
+        glob[g, 1] = 1.0 / total
+
     def combine(g):
         @pl.when(me == stat_owner(g))
         def _():
             drain(stat_in.at[pl.ds(0, n - 1)], tr.at[0])
-            stat_in[me] = stat[g]
-            top = stat_in[0, 0]
-            for d in range(1, n):
-                top = jnp.maximum(top, stat_in[d, 0])
-            total = jnp.zeros_like(top)
-            for d in range(n):
-                total = total + stat_in[d, 1] * jnp.exp(stat_in[d, 0] - top)
-            glob[g, 0] = top
-            glob[g, 1] = 1.0 / total
+            join(g, stat_in)
 
             @pl.loop(1, n)
             def _(k):
@@ -163,7 +167,7 @@
             sum8 = jnp.zeros((8, chunk), jnp.float32)
             for t in range(positions // tblk):
                 s = ebuf[g, t * tblk:(t + 1) * tblk, lanes]
-                e = jnp.exp((s - top) * scale)
+                e = jnp.exp2((s - top) * (scale * LOG2E))
                 ebuf[g, t * tblk:(t + 1) * tblk, lanes] = e
                 sum8 = sum8 + jnp.sum(e.reshape(tblk // 8, 8, chunk), axis=0)
             total = jnp.sum(sum8, axis=0, keepdims=True)
@@ -174,15 +178,25 @@
 
         dest = stat_owner(g)
 
-        @pl.when(me != dest)
+        @pl.when((g < G - 1) & (me != dest))
         def _():
             remote(stat.at[g], stat_in.at[me], ts.at[g], tr.at[0], dest).start()
 
+        @pl.when(g == G - 1)
+        def _():
+            @pl.loop(1, n)
+            def _(k):
+                remote(stat.at[g], stat_all.at[me], es.at[0], er.at[0], lax.rem(me + k, n)).start()
+
+    rows3 = rows_send.reshape(n, cap_pad, 2 * HEAD_DIM)
+    own_rows = pltpu.make_async_copy(rows3.at[me], rows_out.at[me], ls.at[3])
+    own_rows.start()
     mid_peer = a * 4 + (1 - b) * 2 + c
     core_peer = a * 4 + b * 2 + (1 - c)
-    lag = 3
-
-    @pl.loop(0, G + lag)
+
+    lag = 5
+
+    @pl.loop(0, G + 2)
     def _(step):
         @pl.when(step < G)
         def _():
@@ -190,6 +204,13 @@
             drain(qall.at[g, c, b, pl.ds(0, A - 1)], zr.at[g])
             remote(qall.at[g, c, b], qall.at[g, c, b], ys.at[g], yr.at[g], mid_peer).start()
 
+        @pl.when(step == G // 2)
+        def _():
+            @pl.loop(1, n)
+            def _(k):
+                peer = lax.rem(me + k, n)
+                remote(rows3.at[peer], rows_out.at[me], rs.at[0], rr.at[0], peer).start()
+
         @pl.when((step >= 1) & (step < G + 1))
         def _():
             g = step - 1
@@ -202,27 +223,26 @@
             drain(qall.at[g, 1 - c], br.at[g])
             compute(g)
 
-        @pl.when(step >= 3)
-        def _():
-            combine(step - 3)
-
-    rows3 = rows_send.reshape(n, cap_pad, 2 * HEAD_DIM)
-
-    @pl.loop(1, n)
-    def _(k):
-        peer = lax.rem(me + k, n)
-        remote(rows3.at[peer], rows_out.at[me], rs.at[0], rr.at[0], peer).start()
-
-    own_rows = pltpu.make_async_copy(rows3.at[me], rows_out.at[me], ls.at[3])
-    own_rows.start()
+        @pl.when(step >= lag)
+        def _():
+            combine(step - lag)
+
+    @pl.loop(G + 2 - lag, G - 1)
+    def _(g):
+        combine(g)
 
     ones = jnp.ones((8, LANES), jnp.float32)
 
     @pl.loop(0, G)
     def _(g):
-        @pl.when(me != stat_owner(g))
+        @pl.when((g < G - 1) & (me != stat_owner(g)))
         def _():
             drain(glob.at[g], gr.at[g])
+
+        @pl.when(g == G - 1)
+        def _():
+            drain(stat_all.at[pl.ds(0, n - 1)], er.at[0])
+            join(g, stat_all)
 
         weight = jnp.exp(stat[g, 0] - glob[g, 0]) * glob[g, 1]
         for t in range(positions // LANES):
@@ -296,11 +316,11 @@
         drain(qall.at[g, c, b], ys.at[g])
         drain(qall.at[g, c], bs.at[g])
 
-        @pl.when(me != stat_owner(g))
+        @pl.when((g < G - 1) & (me != stat_owner(g)))
         def _():
             drain(stat.at[g], ts.at[g])
 
-        @pl.when(me == stat_owner(g))
+        @pl.when((g < G - 1) & (me == stat_owner(g)))
         def _():
             drain(stat_in.at[pl.ds(0, n - 1)], gs.at[0])
 
@@ -312,10 +332,25 @@
     def _():
         drain(halo.at[5], hs.at[1])
 
+    drain(stat_all.at[pl.ds(0, n - 1)], es.at[0])
     drain(ssend.at[pl.ds(0, n - 1)], ss.at[0])
     drain(srecv.at[pl.ds(0, n - 1)], sr.at[0])
     srecv[me] = ssend[me]
     score_out[...] = srecv[...]
+
+
+def finish(cap, imp_in, rows_in, score_in, imp_ref, rows_ref, score_ref):
+    n = rows_in.shape[0]
+    imp_ref[...] = imp_in[...]
+    rows_ref[...] = rows_in[:, 0:cap, :]
+    table = jnp.concatenate([score_in[k] for k in range(n)], axis=0).astype(jnp.bfloat16)
+    column = iota((LANES, n * cap), 1) - iota((LANES, n * cap), 0)
+    unfold = jnp.where(column % cap == 0, 1.0, 0.0)
+    unfold = jnp.where(iota((LANES, n * cap), 0) < cap, unfold, 0.0).astype(jnp.bfloat16)
+    wide = jnp.dot(table, unfold, preferred_element_type=jnp.float32)
+    within = iota((n, n * cap), 1) - iota((n, n * cap), 0) * cap
+    line = jnp.sum(jnp.where((within >= 0) & (within < cap), wide, 0.0), axis=0, keepdims=True)
+    score_ref[...] = line.astype(jnp.bfloat16).reshape(n * cap)
 
 
 def per_device(n, cached_keys, cached_values, window_queries, kept_count, kept_entry, row_owner):
@@ -356,6 +391,7 @@
             pltpu.VMEM((KV_HEADS, positions, n * qrows), f32),
             pltpu.VMEM((KV_HEADS, 2, lane_rows, LANES), f32),
             pltpu.VMEM((n, 2, lane_rows, LANES), f32),
+            pltpu.VMEM((n, 2, lane_rows, LANES), f32),
             pltpu.VMEM((KV_HEADS, 2, lane_rows, LANES), f32),
             pltpu.VMEM((n * cap_pad, 2 * HEAD_DIM), bf16),
             pltpu.VMEM((n * cap_pad, positions), bf16),
@@ -367,17 +403,24 @@
         ]
         + [dma((KV_HEADS,))] * 6
         + [dma((KV_HEADS,)), dma((1,)), dma((1,)), dma((KV_HEADS,)), dma((1,)), dma((1,))]
-        + [dma((2,)), dma((2,)), dma((1,)), dma((1,)), dma((4,))],
+        + [dma((2,)), dma((2,)), dma((1,)), dma((1,)), dma((4,)), dma((1,)), dma((1,))],
         compiler_params=pltpu.CompilerParams(
             collective_id=0, has_side_effects=True, vmem_limit_bytes=60 * 1024 * 1024
         ),
         name="snap",
-    )(cached_keys, cached_values, wq, kept_count, kept_entry.reshape(1, slots), row_owner.reshape(1, slots))
-    return (
-        importance,
-        rows[:, :cap].reshape(n * cap, 2 * HEAD_DIM),
-        score[:, 0, :cap].reshape(n * cap).astype(bf16),
-    )
+    )(cached_keys, cached_values, wq, kept_count, kept_entry, row_owner)
+    importance, rows, score = pl.pallas_call(
+        functools.partial(finish, cap),
+        out_shape=(
+            jax.ShapeDtypeStruct((KV_HEADS, positions), f32),
+            jax.ShapeDtypeStruct((n, cap, 2 * HEAD_DIM), bf16),
+            jax.ShapeDtypeStruct((n * cap,), bf16),
+        ),
+        in_specs=[vmem, vmem, vmem],
+        out_specs=(vmem, vmem, vmem),
+        name="finish",
+    )(importance, rows, score)
+    return importance, rows.reshape(n * cap, 2 * HEAD_DIM), score
 
 
 def solution(mesh):

time: 67.3 us -> 58.6 us (0.87)
  local copies, waits for them, and re-layouts: 7.03 us -> 0 us
  Pallas kernels: 58.6 us -> 57.1 us
    pallas_call x1, Pallas kernels: 58.6 us -> 55.3 us  [per_device(): pl.pallas_call(functools.partial(kernel, n, cap, cap_pad, pool_scale), ou...]
    reshape x2 -> x0, local copies, waits for them, and re-layouts: 2.53 us -> none  [the longest x1 1.27 us: per_device(): kept_entry.reshape(1, slots)]
    slice x2 -> x0, local copies, waits for them, and re-layouts: 2.45 us -> none  [the longest x1 1.72 us: per_device(): rows[:, :cap].reshape(n * cap, 2 * HEAD_DIM)]
    pallas_call x0 -> x1, Pallas kernels: none -> 1.79 us  [per_device(): pl.pallas_call(functools.partial(finish, cap), out_shape=(jax.ShapeDtypeS...]
    unnamed x1 -> x0, local copies, waits for them, and re-layouts: 1.37 us -> none
    convert_element_type x1 -> x0, local copies, waits for them, and re-layouts: 0.68 us -> none  [per_device(): score[:, 0, :cap].reshape(n * cap).astype(bf16)]
where the time goes in v2:
time: 58.6 us; the launch traced here: 58.4 us
  Pallas kernels  57.1 us (97%)
  between operations  1.29 us (2%)
    pallas_call x1, Pallas kernels, per_device(): pl.pallas_call(functools.partial(kernel, n, cap, cap_pad, pool_scale), ou...  55.3 us
    pallas_call x1, Pallas kernels, per_device(): pl.pallas_call(functools.partial(finish, cap), out_shape=(jax.ShapeDtypeS...  1.79 us

profile of v2, /device:TPU:0, one launch (start us, length us, event | category | flops | bytes accessed | tf_op | source)
XLA Modules:
  0.0 58.4 jit_solution(11042464434979427484)
XLA Ops:
  1.3 55.3 %snap.1 = (f32[8,1024]{1,0:T(8,128)}, bf16[16,48,256]{2,1,0:T(8,128)(2,1)}, f32[16,1,128]{2,1,0:T(1,128)}) custom-call(bf16[1024,1024]{1,0:T(8,128)(2,1)} %keys_hbm.1, bf16[1024,1024]{1,0:T(8,128)(2,1)} %vals_hbm.1, bf16[8,64,128]{2,1,0:T(8,128)(2,1)} %bitcast.6, s32[1]{0:T(128)S(6)} %copy.9.count_ref, s32[640]{0:T(1024)} %entry_ref.1, s32[640]{0:T(1024)} %owner_ref.1), custom_call_target="tpu_custom_call" | custom-call | tf_op jit(solution)/shard_map/snap/pallas_call | solution.py:378
  56.6 1.8 %finish.1 = (f32[8,1024]{1,0:T(8,128)}, bf16[16,40,256]{2,1,0:T(8,128)(2,1)}, bf16[640]{0:T(1024)(128)(2,1)}) custom-call(f32[8,1024]{1,0:T(8,128)} %get-tuple-element.9.imp_in, bf16[16,48,256]{2,1,0:T(8,128)(2,1)} %get-tuple-element.10.rows_in, f32[16,1,128]{2,1,0:T(1,128)} %get-tuple-element.11.score_in), custom_call_target="tpu_custom_call" | custom-call | tf_op jit(solution)/shard_map/finish/pallas_call | solution.py:412
